TPU v7x, 32 devices: a whole 2x2x4 slice. The times are simulated.
32 devices in a mesh: row: 8 (over z, core), col: 4 (over y, x).
Axes of the slice: x: 2, y: 2, z: 4, core: 2. Of those that a mesh axis runs over, the one named last changes fastest.
Arguments:
- roll_hidden: bfloat16 [1344, 4096], P(('row', 'col')), may hold values from -6 to 6
- roll_cotangent: bfloat16 [1344, 4096], P(('row', 'col')), may hold values from -6 to 6
- lengths: int32 [32], P(('row', 'col')), may hold values from 1 to 42, as said below
- owners: int32 [32], P(('row', 'col')), may hold values from 0 to 7, as said below
- prompts: int32 [32], P(('row', 'col')), may hold values from 0 to 3
- rewards: float32 [32], P(('row', 'col')), may hold values from -5 to 5
- gate_weight: bfloat16 [4096, 14784], P('col', 'row'), may hold values from -0.09375 to 0.09375
- up_weight: bfloat16 [4096, 14784], P('col', 'row'), may hold values from -0.09375 to 0.09375
- down_weight: bfloat16 [14784, 4096], P('row', 'col'), may hold values from -0.046875 to 0.046875
Outputs:
- grad_input: bfloat16 [1024, 4096], P('row', 'col')
- grad_gate: bfloat16 [4096, 14784], P('col', 'row')
- grad_up: bfloat16 [4096, 14784], P('col', 'row')
- grad_down: bfloat16 [14784, 4096], P('row', 'col')
Inputs may be any that keep to these rules, and one draw needn't show every extreme that they name: `owners`: each owner value names exactly 4 rows; the lengths of one owner's rows sum to at most 128, and to exactly 128 for some owner in every draw. `lengths`: some row has length 42 in every draw.
All inputs are finite; a program needn't handle non-finite values.
Results may differ from a plain program's by a relative error of at most 0.025.
Values may be sent and summed in bfloat16 or wider, within the bound.
A program may use at most 128 MiB of HBM per device.

v0:
```python
import jax
import jax.numpy as jnp
from jax import lax
from jax.sharding import PartitionSpec as P

CAPR = 128


spread_floor = 0.7


def row_weights(lengths, prompts, rewards, count_prompts):
    onehot = (prompts[:, None] == jnp.arange(count_prompts, dtype=jnp.int32)[None, :]).astype(
        jnp.float32
    )
    counts = jnp.maximum(jnp.sum(onehot, 0), 1.0)
    means = jnp.sum(onehot * rewards[:, None], 0) / counts
    centred = rewards - jnp.sum(onehot * means[None, :], 1)
    spreads = jnp.sqrt(jnp.sum(onehot * (centred * centred)[:, None], 0) / counts)
    divisor = jnp.maximum(jnp.sum(onehot * spreads[None, :], 1), spread_floor)
    return centred / divisor / lengths.astype(jnp.float32)


def row_offsets(lengths, owners):
    count = lengths.shape[0]
    places = jnp.arange(count, dtype=jnp.int32)
    earlier = (owners[None, :] == owners[:, None]) & (places[None, :] < places[:, None])
    return jnp.sum(jnp.where(earlier, lengths[None, :], 0), 1)


def source_index(lengths, owners, offsets, slot_count, capacity, total):
    count = lengths.shape[0]
    slots = jnp.arange(slot_count, dtype=jnp.int32)
    live = slots[None, :] < lengths[:, None]
    target = jnp.where(live, owners[:, None] * capacity + offsets[:, None] + slots[None, :], total)
    flat_source = slots[None, :] * count + jnp.arange(count, dtype=jnp.int32)[:, None]
    empty = jnp.full((total,), slot_count * count, jnp.int32)
    return empty.at[target.reshape(-1)].set(flat_source.reshape(-1), mode="drop")


def per_device(
    roll_hidden,
    roll_cotangent,
    lengths,
    owners,
    prompts,
    rewards,
    gate_weight,
    up_weight,
    down_weight,
):
    row_count = lax.axis_size("row")
    col_count = lax.axis_size("col")
    total_tokens = row_count * CAPR
    count_prompts = row_count * col_count // 8
    slot_count = roll_hidden.shape[0]
    width = roll_hidden.shape[1] // col_count
    local = jnp.stack(
        [
            lengths.astype(jnp.float32),
            owners.astype(jnp.float32),
            prompts.astype(jnp.float32),
            rewards,
        ],
        axis=1,
    )
    table = lax.all_gather(local, ("row", "col"), axis=0, tiled=True)
    all_lengths = table[:, 0].astype(jnp.int32)
    all_owners = table[:, 1].astype(jnp.int32)
    all_prompts = table[:, 2].astype(jnp.int32)
    weights = row_weights(all_lengths, all_prompts, table[:, 3], count_prompts)
    offsets = row_offsets(all_lengths, all_owners)
    mine = lax.dynamic_slice_in_dim(weights, lax.axis_index(("row", "col")), 1, 0)
    live = (jnp.arange(slot_count, dtype=jnp.int32) < lengths[0])[:, None]
    upstream = jnp.where(live, roll_cotangent.astype(jnp.float32) * mine[0], 0.0).astype(
        jnp.bfloat16
    )
    hidden_blocks = roll_hidden.reshape(slot_count, col_count, width)
    upstream_blocks = upstream.reshape(slot_count, col_count, width)
    hidden_cols, upstream_cols = (
        lax.all_to_all(hidden_blocks, "col", split_axis=1, concat_axis=1, tiled=True),
        lax.all_to_all(upstream_blocks, "col", split_axis=1, concat_axis=1, tiled=True),
    )
    hidden_all, upstream_all = (
        lax.all_gather(hidden_cols, "row", axis=1, tiled=True),
        lax.all_gather(upstream_cols, "row", axis=1, tiled=True),
    )
    sources = source_index(all_lengths, all_owners, offsets, slot_count, CAPR, total_tokens)
    packed = jnp.take(hidden_all.reshape(-1, width), sources, axis=0, mode="fill", fill_value=0)
    packed_grad = jnp.take(
        upstream_all.reshape(-1, width), sources, axis=0, mode="fill", fill_value=0
    )
    gate_term = jnp.dot(packed, gate_weight, preferred_element_type=jnp.float32)
    up_term = jnp.dot(packed, up_weight, preferred_element_type=jnp.float32)
    gate, upval = (
        lax.psum(gate_term.astype(jnp.bfloat16), "col").astype(jnp.float32),
        lax.psum(up_term.astype(jnp.bfloat16), "col").astype(jnp.float32),
    )
    sig = jax.nn.sigmoid(gate)
    silu = gate * sig
    hidden = (silu * upval).astype(jnp.bfloat16)
    contract_cols = (((1,), (1,)), ((), ()))
    grad_term = lax.dot_general(
        packed_grad, down_weight, contract_cols, preferred_element_type=jnp.float32
    )
    grad_hidden = lax.psum(grad_term.astype(jnp.bfloat16), "col").astype(jnp.float32)
    grad_gate_act = (grad_hidden * upval * sig * (1.0 + gate * (1.0 - sig))).astype(jnp.bfloat16)
    grad_up_act = (grad_hidden * silu).astype(jnp.bfloat16)
    contract_rows = (((0,), (0,)), ((), ()))
    grad_down = lax.dot_general(
        hidden, packed_grad, contract_rows, preferred_element_type=jnp.float32
    ).astype(jnp.bfloat16)
    grad_gate = lax.dot_general(
        packed, grad_gate_act, contract_rows, preferred_element_type=jnp.float32
    ).astype(jnp.bfloat16)
    grad_up = lax.dot_general(
        packed, grad_up_act, contract_rows, preferred_element_type=jnp.float32
    ).astype(jnp.bfloat16)
    term = lax.dot_general(
        grad_gate_act, gate_weight, contract_cols, preferred_element_type=jnp.float32
    )
    grad_input = lax.psum_scatter(
        (
            term
            + lax.dot_general(
                grad_up_act, up_weight, contract_cols, preferred_element_type=jnp.float32
            )
        ).astype(jnp.bfloat16),
        "row",
        scatter_dimension=0,
        tiled=True,
    )
    return (grad_input, grad_gate, grad_up, grad_down)


def solution(mesh):
    return jax.shard_map(
        per_device,
        mesh=mesh,
        in_specs=(
            P(("row", "col"), None),
            P(("row", "col"), None),
            P(("row", "col")),
            P(("row", "col")),
            P(("row", "col")),
            P(("row", "col")),
            P("col", "row"),
            P("col", "row"),
            P("row", "col"),
        ),
        out_specs=(P("row", "col"), P("col", "row"), P("col", "row"), P("row", "col")),
        check_vma=False,
    )
```

profile of v0, /device:TPU:0, one launch (start us, length us, event | category | flops | bytes accessed | tf_op | source)
XLA Modules:
  0.0 450.1 jit_solution(12010402054570381515)
XLA Ops:
  7.2 0.0 all-gather.6.cloned.1.call-start
  7.2 1.2 reshape.123
  8.4 0.1 copy.25
  8.5 12.2 %all_to_all.10 = bf16[42,4,1024]{2,0,1:T(8,128)(2,1)} all-to-all(bf16[42,4,1024]{2,0,1:T(8,128)(2,1)S(1)} %copy.25), channel_id=1, replica_groups=mesh['row'=8,'col'=4] {'col'}, dimensions={1} | all-to-all | bytes 688128 | tf_op jit(solution)/shard_map/all_to_all | solution.py:81
  20.7 0.0 all-gather.6.cloned.1.call-update
  20.8 0.0 all-gather.4.cloned.1.call-start
  23.4 0.1 maximum_bitcast_fusion
  23.5 66.8 %all-gather = f32[32,1,4]{2,1,0:T(1,128)S(1)} all-gather(f32[1,1,4]{2,1,0:T(1,128)S(1)} %maximum_bitcast_fusion), channel_id=1, replica_groups=mesh['row'=8,'col'=4] {'row','col'}, dimensions={0}, use_global_device_ids=true | all-gather | bytes 528 | tf_op jit(solution)/shard_map/all_gather | solution.py:67
  90.2 0.1 copy.22
  90.3 0.2 convert_reduce_fusion
  90.5 0.1 select_reduce_fusion.3
  90.6 0.1 select_reduce_fusion.2
  90.7 0.1 select_reduce_fusion.1
  90.8 0.6 dynamic_slice.3
  91.4 1.8 select_convert_fusion
  93.2 0.2 reshape.121
  93.4 0.1 copy.23
  93.5 9.5 %all_to_all.11 = bf16[42,4,1024]{2,0,1:T(8,128)(2,1)} all-to-all(bf16[42,4,1024]{2,0,1:T(8,128)(2,1)S(1)} %copy.23), channel_id=1, replica_groups=mesh['row'=8,'col'=4] {'col'}, dimensions={1} | all-to-all | bytes 688128 | tf_op jit(solution)/shard_map/all_to_all | solution.py:82
  103.0 0.0 all-gather.4.cloned.1.call-update
  103.0 0.0 all-reduce.3.cloned.1.call-start
  103.1 0.1 reshape.145
  103.2 0.2 select_reduce_fusion
  103.4 0.1 add_select_fusion
  103.5 0.1 select_n.47
  103.6 7.6 %scatter_custom_fusion = s32[1024]{0:T(1024)S(1)} fusion(s32[1344]{0:T(1024)S(1)} %fusion.15, s32[1344]{0:T(1024)S(1)} %reshape.145, s32[]{:T(128)} %constant.14.clone.1), kind=kCustom, calls=%fused_computation.40 | custom fusion | bytes 4100 | tf_op jit(solution)/shard_map/scatter | solution.py:38
  111.3 0.0 all-gather.6.cloned.1.call-done
  111.3 3.4 copy.26
  114.7 5.5 %gather_fusion.1 = bf16[1024,1024]{1,0:T(8,128)(2,1)} fusion(bf16[1344,1024]{1,0:T(8,128)(2,1)S(1)} %bitcast.48, s32[1024]{0:T(1024)S(1)} %fusion.16), kind=kCustom, calls=%fused_computation.1.clone | custom fusion | bytes 4198400 | tf_op jit(solution)/shard_map/jit(_take)/gather | solution.py:89
  120.2 17.9 %all-gather.4.cloned.1.call-done = bf16[42,32,1024]{2,0,1:T(8,128)(2,1)} async-done(((bf16[42,4,1024]{2,0,1:T(8,128)(2,1)}), bf16[42,32,1024]{2,0,1:T(8,128)(2,1)}) %all-gather.4.cloned.1.call-update) | async-done | bytes 2752528 | tf_op jit(solution)/shard_map/all_gather | solution.py:86
  138.1 3.4 copy.24
  141.5 5.4 %gather_fusion = bf16[1024,1024]{1,0:T(8,128)(2,1)} fusion(bf16[1344,1024]{1,0:T(8,128)(2,1)S(1)} %bitcast.47, s32[1024]{0:T(1024)S(1)} %fusion.16), kind=kCustom, calls=%fused_computation.clone | custom fusion | bytes 4198400 | tf_op jit(solution)/shard_map/jit(_take)/gather | solution.py:90
  146.8 0.0 copy-start.6
  146.8 8.9 %convolution_convert_fusion.2 = bf16[1024,1848]{0,1:T(8,128)(2,1)} fusion(bf16[1024,1848]{0,1:T(8,128)(2,1)} %param.17, bf16[1024,1024]{1,0:T(8,128)(2,1)} %gather_fusion.1, pred[1024]{0:T(1024)(128)(4,1)S(1)} %compare_and_fusion), kind=kOutput, calls=%fused_computation.23 | convolution fusion | flops 3878477824 | bytes 9667584 | tf_op jit(solution)/shard_map/dot_general | solution.py:93
  155.8 0.0 copy-done.6
  155.8 0.0 copy-done.11
  155.8 0.0 copy-start.9
  155.8 6.3 %convolution_convert_fusion.3 = bf16[1024,1848]{0,1:T(8,128)(2,1)} fusion(bf16[1024,1848]{0,1:T(8,128)(2,1)S(1)} %copy-done.11, bf16[1024,1024]{1,0:T(8,128)(2,1)S(1)} %copy-done.6, pred[1024]{0:T(1024)(128)(4,1)S(1)} %compare_and_fusion), kind=kOutput, calls=%fused_computation.24 | convolution fusion | flops 3878477824 | bytes 9667584 | tf_op jit(solution)/shard_map/dot_general | solution.py:94
  162.2 0.0 copy-done.7
  162.2 0.0 copy-done.9
  162.2 6.3 %convolution_convert_fusion.4 = bf16[1024,1848]{0,1:T(8,128)(2,1)} fusion(bf16[1848,1024]{1,0:T(8,128)(2,1)S(1)} %copy-done.9, bf16[1024,1024]{1,0:T(8,128)(2,1)S(1)} %copy-done.7, pred[1024]{0:T(1024)(128)(4,1)S(1)} %compare_and_fusion), kind=kOutput, calls=%fused_computation.25 | convolution fusion | flops 3878477824 | bytes 9667584 | tf_op jit(solution)/shard_map/dot_general | solution.py:103
  168.5 0.0 all-reduce.3.cloned.1.call-update
  168.5 0.0 reduce-scatter.2.cloned.1.call-start
  168.6 219.0 %all-reduce.3.cloned.1.call-done = (bf16[1024,1848]{0,1:T(8,128)(2,1)}, bf16[1024,1848]{0,1:T(8,128)(2,1)}, bf16[1024,1848]{0,1:T(8,128)(2,1)}) async-done(((bf16[1024,1848]{0,1:T(8,128)(2,1)}, bf16[1024,1848]{0,1:T(8,128)(2,1)}, bf16[1024,1848]{0,1:T(8,128)(2,1)}), (bf16[1024,1848]{0,1:T(8,128)(2,1)}, bf16[1024,1848]{0,1:T(8,128)(2,1)}, bf16[1024,1848]{0,1:T(8,128)(2,1)})) %all-reduce.3.cloned.1.call-update) | async-done | bytes 11354128 | tf_op jit(solution)/shard_map/psum | solution.py:97
  387.5 6.3 %fusion.3 = bf16[1024,1848]{0,1:T(8,128)(2,1)S(1)} fusion(bf16[1024,1848]{0,1:T(8,128)(2,1)} %get-tuple-element.7, bf16[1024,1848]{0,1:T(8,128)(2,1)} %get-tuple-element.8, bf16[1024,1848]{0,1:T(8,128)(2,1)} %get-tuple-element.9), kind=kLoop, calls=%fused_computation.12 | loop fusion | flops 24600576 | bytes 15138816 | tf_op jit(solution)/shard_map/convert_element_type | solution.py:107
  393.8 0.0 copy-start.5
  393.8 1.9 copy-done.5
  395.7 0.0 copy-done.10
  395.7 4.7 %fusion.27 = f32[1024,1024]{1,0:T(8,128)S(1)} fusion(bf16[1024,1848]{0,1:T(8,128)(2,1)S(1)} %fusion.3, bf16[1024,1848]{0,1:T(8,128)(2,1)S(1)} %copy-done.10), kind=kOutput, calls=%fused_computation.66 | convolution fusion | flops 3875536896 | bytes 11763712 | tf_op jit(solution)/shard_map/dot_general | solution.py:119
  400.5 0.0 copy-done.1
  400.5 0.0 copy-done.3
  400.5 0.0 copy-done.12
  400.5 6.3 %add_convert_fusion = bf16[1024,1024]{1,0:T(8,128)(2,1)} fusion(f32[1024,1024]{1,0:T(8,128)S(1)} %fusion.27, bf16[1024,1848]{0,1:T(8,128)(2,1)S(1)} %copy-done.12, bf16[1024,1848]{0,1:T(8,128)(2,1)S(1)} %copy-done.3, bf16[1024,1848]{0,1:T(8,128)(2,1)S(1)} %copy-done.1), kind=kOutput, calls=%fused_computation.18 | convolution fusion | flops 3892772864 | bytes 17645568 | tf_op jit(solution)/shard_map/dot_general | solution.py:125
  406.8 0.0 reduce-scatter.2.cloned.1.call-update
  406.8 0.0 copy-start.2
  406.8 0.0 copy-start.4
  406.8 7.9 %convolution_convert_fusion.1 = bf16[1024,1848]{0,1:T(8,128)(2,1)} fusion(bf16[1024,1848]{0,1:T(8,128)(2,1)} %copy-done.5, bf16[1024,1024]{1,0:T(8,128)(2,1)S(1)} %copy-done.6, pred[1024]{0:T(1024)(128)(4,1)S(1)} %compare_and_fusion), kind=kOutput, calls=%fused_computation.22 | convolution fusion | flops 3878477824 | bytes 9667584 | tf_op jit(solution)/shard_map/dot_general | solution.py:113
  414.7 0.0 copy-done.2
  414.7 0.0 copy-done.4
  414.7 0.0 copy-start.8
  414.7 6.4 %convolution_convert_fusion = bf16[1024,1848]{0,1:T(8,128)(2,1)} fusion(bf16[1024,1024]{1,0:T(8,128)(2,1)S(1)} %copy-done.6, pred[1024]{0:T(1024)(128)(4,1)S(1)} %compare_and_fusion, bf16[1024,1848]{0,1:T(8,128)(2,1)S(1)} %copy-done.4, bf16[1024,1848]{0,1:T(8,128)(2,1)S(1)} %copy-done.2), kind=kOutput, calls=%fused_computation.21 | convolution fusion | flops 3893616640 | bytes 13452288 | tf_op jit(solution)/shard_map/dot_general | solution.py:116
  421.2 0.0 copy-done
  421.2 0.0 copy-done.8
  421.2 6.4 %fusion.11 = bf16[1848,1024]{1,0:T(8,128)(2,1)} fusion(bf16[1024,1848]{0,1:T(8,128)(2,1)S(1)} %copy-done, bf16[1024,1848]{0,1:T(8,128)(2,1)S(1)} %copy-done.2, bf16[1024,1024]{1,0:T(8,128)(2,1)S(1)} %copy-done.8, pred[1024]{0:T(1024)(128)(4,1)S(1)} %compare_and_fusion), kind=kOutput, calls=%fused_computation.20 | convolution fusion | flops 3893616640 | bytes 13452288 | tf_op jit(solution)/shard_map/dot_general | solution.py:110
  427.6 16.0 %reduce-scatter.2.cloned.1.call-done = bf16[128,1024]{1,0:T(8,128)(2,1)} async-done(((bf16[1024,1024]{1,0:T(8,128)(2,1)}), bf16[128,1024]{1,0:T(8,128)(2,1)}) %reduce-scatter.2.cloned.1.call-update) | async-done | bytes 262160 | tf_op jit(solution)/shard_map/reduce_scatter | solution.py:122
  (19 shorter events, 0.1 us)
Async XLA Ops:
  7.2 104.1 %all-gather.6.cloned.1.call-start = ((), (), s32[]{:S(2)}) async-start(), calls=%async_computation.4 | async-start | bytes 3538944 | tf_op jit(solution)/shard_map/all_gather | solution.py:85
  20.8 117.3 %all-gather.4.cloned.1.call-start = ((), (), s32[]{:S(2)}) async-start(), calls=%async_computation.3 | async-start | bytes 3538944 | tf_op jit(solution)/shard_map/all_gather | solution.py:86
  103.0 284.5 %all-reduce.3.cloned.1.call-start = ((), (), s32[]{:S(2)}) async-start(), calls=%async_computation.6 | async-start | bytes 22708224 | tf_op jit(solution)/shard_map/psum | solution.py:97
  146.8 9.0 %copy-start.6 = (bf16[1024,1024]{1,0:T(8,128)(2,1)S(1)}, bf16[1024,1024]{1,0:T(8,128)(2,1)}, u32[]{:S(2)}) copy-start(bf16[1024,1024]{1,0:T(8,128)(2,1)} %gather_fusion.1) | copy-start | bytes 6291460
  146.8 9.0 %copy-start.11 = (bf16[1024,1848]{0,1:T(8,128)(2,1)S(1)}, bf16[1024,1848]{0,1:T(8,128)(2,1)}, u32[]{:S(2)}) copy-start(bf16[1024,1848]{0,1:T(8,128)(2,1)} %param.18) | copy-start | bytes 11354116
  155.8 6.4 %copy-start.7 = (bf16[1024,1024]{1,0:T(8,128)(2,1)S(1)}, bf16[1024,1024]{1,0:T(8,128)(2,1)}, u32[]{:S(2)}) copy-start(bf16[1024,1024]{1,0:T(8,128)(2,1)} %gather_fusion) | copy-start | bytes 6291460
  155.8 6.4 %copy-start.9 = (bf16[1848,1024]{1,0:T(8,128)(2,1)S(1)}, bf16[1848,1024]{1,0:T(8,128)(2,1)}, u32[]{:S(2)}) copy-start(bf16[1848,1024]{1,0:T(8,128)(2,1)} %param.19) | copy-start | bytes 11354116
  168.5 275.0 %reduce-scatter.2.cloned.1.call-start = ((), (), s32[]{:S(2)}) async-start(), calls=%async_computation.5 | async-start | bytes 2359296 | tf_op jit(solution)/shard_map/reduce_scatter | solution.py:122
  387.5 8.2 %copy-start.10 = (bf16[1024,1848]{0,1:T(8,128)(2,1)S(1)}, bf16[1024,1848]{0,1:T(8,128)(2,1)}, u32[]{:S(2)}) copy-start(bf16[1024,1848]{0,1:T(8,128)(2,1)} %param.17) | copy-start | bytes 11354116
  393.8 1.9 copy-start.5
  395.7 4.8 %copy-start.1 = (bf16[1024,1848]{0,1:T(8,128)(2,1)S(1)}, bf16[1024,1848]{0,1:T(8,128)(2,1)}, u32[]{:S(2)}) copy-start(bf16[1024,1848]{0,1:T(8,128)(2,1)} %get-tuple-element.9) | copy-start | bytes 11354116
  395.7 4.8 %copy-start.3 = (bf16[1024,1848]{0,1:T(8,128)(2,1)S(1)}, bf16[1024,1848]{0,1:T(8,128)(2,1)}, u32[]{:S(2)}) copy-start(bf16[1024,1848]{0,1:T(8,128)(2,1)} %get-tuple-element.8) | copy-start | bytes 11354116
  395.7 4.8 %copy-start.12 = (bf16[1024,1848]{0,1:T(8,128)(2,1)S(1)}, bf16[1024,1848]{0,1:T(8,128)(2,1)}, u32[]{:S(2)}) copy-start(bf16[1024,1848]{0,1:T(8,128)(2,1)} %param.18) | copy-start | bytes 11354116
  406.8 7.9 %copy-start.2 = (bf16[1024,1848]{0,1:T(8,128)(2,1)S(1)}, bf16[1024,1848]{0,1:T(8,128)(2,1)}, u32[]{:S(2)}) copy-start(bf16[1024,1848]{0,1:T(8,128)(2,1)} %get-tuple-element.9) | copy-start | bytes 11354116
  406.8 7.9 %copy-start.4 = (bf16[1024,1848]{0,1:T(8,128)(2,1)S(1)}, bf16[1024,1848]{0,1:T(8,128)(2,1)}, u32[]{:S(2)}) copy-start(bf16[1024,1848]{0,1:T(8,128)(2,1)} %get-tuple-element.8) | copy-start | bytes 11354116
  414.7 6.4 %copy-start = (bf16[1024,1848]{0,1:T(8,128)(2,1)S(1)}, bf16[1024,1848]{0,1:T(8,128)(2,1)}, u32[]{:S(2)}) copy-start(bf16[1024,1848]{0,1:T(8,128)(2,1)} %get-tuple-element.7) | copy-start | bytes 11354116
  414.7 6.4 %copy-start.8 = (bf16[1024,1024]{1,0:T(8,128)(2,1)S(1)}, bf16[1024,1024]{1,0:T(8,128)(2,1)}, u32[]{:S(2)}) copy-start(bf16[1024,1024]{1,0:T(8,128)(2,1)} %gather_fusion) | copy-start | bytes 6291460
Sparse Core Ops, SparseCore 0:
  20.9 37.9 all-gather.5
  103.1 34.8 all-gather.3
  168.6 218.8 all-reduce.2
  406.9 36.5 reduce-scatter.1
where the time goes:
time: 450 us
  waiting for transfers between devices  253 us (56%)
  blocking collectives  88.5 us (20%)
  matrix products  53.4 us (12%)
  local copies, waits for them, and re-layouts  29.7 us (7%)
  between operations  16.6 us (4%)
  other arithmetic  8.91 us (2%)
    psum x1, waiting for transfers between devices, per_device(): lax.psum(up_term.astype(jnp.bfloat16), 'col').astype(jnp.float32)  219 us
    all_gather x1, blocking collectives, per_device(): table = lax.all_gather(local, ('row', 'col'), axis=0, tiled=True)  66.8 us
    all_gather x1, waiting for transfers between devices, per_device(): lax.all_gather(upstream_cols, 'row', axis=1, tiled=True)  17.9 us
    reduce_scatter x1, waiting for transfers between devices, per_device(): lax.psum_scatter((term + lax.dot_general(grad_up_act, up_weight, contract...  16 us
    all_to_all x1, blocking collectives, per_device(): lax.all_to_all(hidden_blocks, 'col', split_axis=1, concat_axis=1, tiled=T...  12.2 us
    all_to_all x1, blocking collectives, per_device(): lax.all_to_all(upstream_blocks, 'col', split_axis=1, concat_axis=1, tiled...  9.51 us
  transfers between devices with their start and end apart: 4, of which 3 were waited for; matrix products, arithmetic and copies ran while one was open for 9% of the time, Pallas kernels for 0%

commit v1 on v0

--- a/solution.py
+++ b/solution.py
@@ -1,9 +1,15 @@
+import functools
+
 import jax
 import jax.numpy as jnp
 from jax import lax
+from jax.experimental import pallas as pl
+from jax.experimental.pallas import tpu as pltpu
 from jax.sharding import PartitionSpec as P
 
 CAPR = 128
+MESH = pl.DeviceIdType.MESH
+CHUNK = 256
 
 
 spread_floor = 0.7
@@ -28,14 +34,152 @@
     return jnp.sum(jnp.where(earlier, lengths[None, :], 0), 1)
 
 
-def source_index(lengths, owners, offsets, slot_count, capacity, total):
-    count = lengths.shape[0]
-    slots = jnp.arange(slot_count, dtype=jnp.int32)
-    live = slots[None, :] < lengths[:, None]
-    target = jnp.where(live, owners[:, None] * capacity + offsets[:, None] + slots[None, :], total)
-    flat_source = slots[None, :] * count + jnp.arange(count, dtype=jnp.int32)[:, None]
-    empty = jnp.full((total,), slot_count * count, jnp.int32)
-    return empty.at[target.reshape(-1)].set(flat_source.reshape(-1), mode="drop")
+def square_kernel(count, transposed, a_ref, *refs):
+    b_refs, o_refs = refs[:count], refs[count : 2 * count]
+    parts, first_in, second_out, second_in = (
+        refs[2 * count + i * count : 3 * count + i * count] for i in range(4)
+    )
+    send_sem, recv_sem = refs[6 * count :]
+    col = lax.axis_index("col")
+    row = lax.axis_index("row")
+    x, y = lax.rem(col, 2), lax.div(col, 2)
+    x_peer, y_peer = y * 2 + (1 - x), (1 - y) * 2 + x
+    half, quarter, eighth = CHUNK // 2, CHUNK // 4, CHUNK // 8
+    ways = ((x, y, x_peer, y_peer), (y, x, y_peer, x_peer))
+    chunks = a_ref.shape[0] // CHUNK
+
+    barrier = pltpu.get_barrier_semaphore()
+    for peer in (x_peer, y_peer):
+        pl.semaphore_signal(barrier, inc=1, device_id=(row, peer), device_id_type=MESH)
+    pl.semaphore_wait(barrier, 2)
+
+    def rows(start, size):
+        return pl.ds(pl.multiple_of(start, eighth), size)
+
+    def copy(stage, chunk, way, i):
+        f, s, f_peer, s_peer = ways[way]
+        base = chunk * CHUNK + way * half
+        if stage == 0:
+            src = parts[i].at[rows(base + (1 - f) * quarter, quarter)]
+            dst = first_in[i].at[rows(chunk * half + way * quarter, quarter)]
+        elif stage == 1:
+            place = rows(chunk * quarter + way * eighth, eighth)
+            src, dst = second_out[i].at[place], second_in[i].at[place]
+        elif stage == 2:
+            place = rows(base + f * quarter + s * eighth, eighth)
+            src = dst = o_refs[i].at[place]
+        else:
+            place = rows(base + f * quarter, quarter)
+            src = dst = o_refs[i].at[place]
+        return pltpu.make_async_remote_copy(
+            src_ref=src,
+            dst_ref=dst,
+            send_sem=send_sem.at[stage, way, i, chunk],
+            recv_sem=recv_sem.at[stage, way, i, chunk],
+            device_id=(row, f_peer if stage in (0, 3) else s_peer),
+            device_id_type=MESH,
+        )
+
+    def phase_first(chunk, carry):
+        block = a_ref[rows(chunk * CHUNK, CHUNK), :]
+        dims = (((1,), (1 if transposed else 0,)), ((), ()))
+        for i in range(count):
+            parts[i][rows(chunk * CHUNK, CHUNK), :] = lax.dot_general(
+                block, b_refs[i][...], dims, preferred_element_type=jnp.float32
+            ).astype(jnp.bfloat16)
+            for way in range(2):
+                copy(0, chunk, way, i).start()
+        return carry
+
+    def phase_second(chunk, carry):
+        for i in range(count):
+            for way in range(2):
+                f, s = ways[way][:2]
+                copy(0, chunk, way, i).wait_recv()
+                mine = parts[i][
+                    rows(chunk * CHUNK + way * half + f * quarter + (1 - s) * eighth, eighth), :
+                ]
+                other = first_in[i][
+                    rows(chunk * half + way * quarter + (1 - s) * eighth, eighth), :
+                ]
+                second_out[i][rows(chunk * quarter + way * eighth, eighth), :] = (
+                    mine.astype(jnp.float32) + other.astype(jnp.float32)
+                ).astype(jnp.bfloat16)
+                copy(1, chunk, way, i).start()
+        return carry
+
+    def phase_third(chunk, carry):
+        for i in range(count):
+            for way in range(2):
+                f, s = ways[way][:2]
+                copy(1, chunk, way, i).wait_recv()
+                place = rows(chunk * CHUNK + way * half + f * quarter + s * eighth, eighth)
+                mine = parts[i][place, :].astype(jnp.float32)
+                other = first_in[i][
+                    rows(chunk * half + way * quarter + s * eighth, eighth), :
+                ].astype(jnp.float32)
+                pair = second_in[i][rows(chunk * quarter + way * eighth, eighth), :].astype(
+                    jnp.float32
+                )
+                o_refs[i][place, :] = (mine + other + pair).astype(jnp.bfloat16)
+                copy(2, chunk, way, i).start()
+        return carry
+
+    def phase_fourth(chunk, carry):
+        for i in range(count):
+            for way in range(2):
+                copy(2, chunk, way, i).wait_recv()
+                copy(3, chunk, way, i).start()
+        return carry
+
+    def phase_last(chunk, carry):
+        for i in range(count):
+            for way in range(2):
+                copy(3, chunk, way, i).wait_recv()
+                for stage in range(4):
+                    copy(stage, chunk, way, i).wait_send()
+        return carry
+
+    for phase in (phase_first, phase_second, phase_third, phase_fourth, phase_last):
+        lax.fori_loop(0, chunks, phase, 0)
+
+
+def square_sum(a, bs, transposed, collective_id):
+    tokens, depth = a.shape
+    units = bs[0].shape[0 if transposed else 1]
+    count = len(bs)
+    shapes = (tokens, tokens // 2, tokens // 4, tokens // 4)
+    return pl.pallas_call(
+        functools.partial(square_kernel, count, transposed),
+        out_shape=[jax.ShapeDtypeStruct((tokens, units), jnp.bfloat16)] * count,
+        in_specs=[pl.BlockSpec(memory_space=pltpu.VMEM)] * (1 + count),
+        out_specs=[pl.BlockSpec(memory_space=pltpu.VMEM)] * count,
+        scratch_shapes=[
+            pltpu.VMEM((size, units), jnp.bfloat16) for size in shapes for _ in range(count)
+        ]
+        + [pltpu.SemaphoreType.DMA((4, 2, count, tokens // CHUNK))] * 2,
+        compiler_params=pltpu.CompilerParams(
+            collective_id=collective_id, has_side_effects=True, vmem_limit_bytes=56 * 1024 * 1024
+        ),
+        cost_estimate=pl.CostEstimate(
+            flops=2 * count * tokens * depth * units * 6,
+            bytes_accessed=60 * count * tokens * units,
+            transcendentals=0,
+        ),
+    )(a, *bs)
+
+
+def column_sum(a, bs, transposed, collective_id):
+    if lax.axis_size("col") == 4 and a.shape[0] % CHUNK == 0:
+        return square_sum(a, bs, transposed, collective_id)
+    dims = (((1,), (1 if transposed else 0,)), ((), ()))
+    return [
+        lax.psum(
+            lax.dot_general(a, b, dims, preferred_element_type=jnp.float32).astype(jnp.bfloat16),
+            "col",
+        )
+        for b in bs
+    ]
 
 
 def per_device(
@@ -70,40 +214,40 @@
     all_prompts = table[:, 2].astype(jnp.int32)
     weights = row_weights(all_lengths, all_prompts, table[:, 3], count_prompts)
     offsets = row_offsets(all_lengths, all_owners)
-    mine = lax.dynamic_slice_in_dim(weights, lax.axis_index(("row", "col")), 1, 0)
-    live = (jnp.arange(slot_count, dtype=jnp.int32) < lengths[0])[:, None]
-    upstream = jnp.where(live, roll_cotangent.astype(jnp.float32) * mine[0], 0.0).astype(
+    slots = jnp.arange(slot_count, dtype=jnp.int32)
+    target = jnp.where(
+        slots[None, :] < all_lengths[:, None],
+        all_owners[:, None] * CAPR + offsets[:, None] + slots[None, :],
+        total_tokens,
+    ).reshape(-1)
+    slot_weights = jnp.repeat(weights, slot_count)
+    pick = (jnp.arange(total_tokens, dtype=jnp.int32)[:, None] == target[None, :]).astype(
         jnp.bfloat16
     )
-    hidden_blocks = roll_hidden.reshape(slot_count, col_count, width)
-    upstream_blocks = upstream.reshape(slot_count, col_count, width)
-    hidden_cols, upstream_cols = (
-        lax.all_to_all(hidden_blocks, "col", split_axis=1, concat_axis=1, tiled=True),
-        lax.all_to_all(upstream_blocks, "col", split_axis=1, concat_axis=1, tiled=True),
-    )
-    hidden_all, upstream_all = (
-        lax.all_gather(hidden_cols, "row", axis=1, tiled=True),
-        lax.all_gather(upstream_cols, "row", axis=1, tiled=True),
-    )
-    sources = source_index(all_lengths, all_owners, offsets, slot_count, CAPR, total_tokens)
-    packed = jnp.take(hidden_all.reshape(-1, width), sources, axis=0, mode="fill", fill_value=0)
-    packed_grad = jnp.take(
-        upstream_all.reshape(-1, width), sources, axis=0, mode="fill", fill_value=0
-    )
-    gate_term = jnp.dot(packed, gate_weight, preferred_element_type=jnp.float32)
-    up_term = jnp.dot(packed, up_weight, preferred_element_type=jnp.float32)
-    gate, upval = (
-        lax.psum(gate_term.astype(jnp.bfloat16), "col").astype(jnp.float32),
-        lax.psum(up_term.astype(jnp.bfloat16), "col").astype(jnp.float32),
-    )
+
+    def to_cols(rolled):
+        blocks = rolled.reshape(slot_count, col_count, width)
+        return lax.all_to_all(blocks, "col", split_axis=1, concat_axis=0, tiled=True).reshape(
+            col_count * slot_count, width
+        )
+
+    def repack(every):
+        return jnp.dot(pick, every, preferred_element_type=jnp.float32).astype(jnp.bfloat16)
+
+    hidden_cols, table = lax.optimization_barrier((to_cols(roll_hidden), table))
+    hidden_all = lax.all_gather(hidden_cols, "row", axis=0, tiled=True)
+    cotangent_all = lax.all_gather(to_cols(roll_cotangent), "row", axis=0, tiled=True)
+    packed = repack(hidden_all)
+    gate, upval = column_sum(packed, (gate_weight, up_weight), False, 0)
+    packed_grad = repack(
+        (cotangent_all.astype(jnp.float32) * slot_weights[:, None]).astype(jnp.bfloat16)
+    )
+    (grad_hidden,) = column_sum(packed_grad, (down_weight,), True, 1)
+    gate, upval, grad_hidden = (v.astype(jnp.float32) for v in (gate, upval, grad_hidden))
     sig = jax.nn.sigmoid(gate)
     silu = gate * sig
     hidden = (silu * upval).astype(jnp.bfloat16)
     contract_cols = (((1,), (1,)), ((), ()))
-    grad_term = lax.dot_general(
-        packed_grad, down_weight, contract_cols, preferred_element_type=jnp.float32
-    )
-    grad_hidden = lax.psum(grad_term.astype(jnp.bfloat16), "col").astype(jnp.float32)
     grad_gate_act = (grad_hidden * upval * sig * (1.0 + gate * (1.0 - sig))).astype(jnp.bfloat16)
     grad_up_act = (grad_hidden * silu).astype(jnp.bfloat16)
     contract_rows = (((0,), (0,)), ((), ()))

time: 450 us -> 385 us (0.86)
  waiting for transfers between devices: 253 us -> 11 us
  Pallas kernels: 0 us -> 201 us
  local copies, waits for them, and re-layouts: 29.7 us -> 19.5 us
  blocking collectives: 88.5 us -> 79.8 us
  matrix products: 53.4 us -> 46.3 us
    psum x1 -> x0, waiting for transfers between devices: 219 us -> none  [per_device(): lax.psum(up_term.astype(jnp.bfloat16), 'col').astype(jnp.float32)]
    pallas_call x0 -> x2, Pallas kernels: none -> 201 us  [square_sum(): pl.pallas_call(functools.partial(square_kernel, count, transposed), out_s...]
    all_gather x2, waiting for transfers between devices: 17.9 us -> 0.02 us  [the longest x1 0.02 us: per_device(): hidden_all = lax.all_gather(hidden_cols, 'row', axis=0, tiled=True)]
    unnamed x26 -> x22, local copies, waits for them, and re-layouts: 1.92 us -> 14.1 us
    gather x2 -> x0, local copies, waits for them, and re-layouts: 10.9 us -> none  [the longest x1 5.52 us: per_device(): jnp.take(hidden_all.reshape(-1, width), sources, axis=0, mode='fill', fil...]
    all_to_all x2 -> x1, blocking collectives: 21.7 us -> 12.1 us  [to_cols(): lax.all_to_all(blocks, 'col', split_axis=1, concat_axis=0, tiled=True)]
    dot_general x3 -> x2, matrix products: 21.6 us -> 13 us  [repack(): jnp.dot(pick, every, preferred_element_type=jnp.float32)]
    scatter x1 -> x0, local copies, waits for them, and re-layouts: 7.62 us -> none  [source_index(): empty.at[target.reshape(-1)].set(flat_source.reshape(-1), mode='drop')]
  transfers between devices with their start and end apart: 4 -> 4, of which waited for: 3 -> 1; matrix products, arithmetic and copies ran while one was open for 9% -> 12% of each run, Pallas kernels for 0% -> 18%
where the time goes in v1:
time: 385 us; the launch traced here: 384 us
  Pallas kernels  201 us (52%)
  blocking collectives  79.8 us (21%)
  matrix products  46.3 us (12%)
  local copies, waits for them, and re-layouts  19.5 us (5%)
  between operations  16.6 us (4%)
  waiting for transfers between devices  11 us (3%)
  other arithmetic  6.85 us (2%)
    pallas_call x2, Pallas kernels, square_sum(): pl.pallas_call(functools.partial(square_kernel, count, transposed), out_s...  201 us
    all_gather x1, blocking collectives, per_device(): table = lax.all_gather(local, ('row', 'col'), axis=0, tiled=True)  67.7 us
    unnamed x22, local copies, waits for them, and re-layouts  14.1 us
    dot_general x2, matrix products, repack(): jnp.dot(pick, every, preferred_element_type=jnp.float32)  13 us
    all_to_all x1, blocking collectives, to_cols(): lax.all_to_all(blocks, 'col', split_axis=1, concat_axis=0, tiled=True)  12.1 us
    reduce_scatter x1, waiting for transfers between devices, per_device(): lax.psum_scatter((term + lax.dot_general(grad_up_act, up_weight, contract...  11 us
    dot_general x1, matrix products, per_device(): lax.dot_general(packed, grad_gate_act, contract_rows, preferred_element_t...  7.9 us
    dot_general x1, matrix products, per_device(): lax.dot_general(hidden, packed_grad, contract_rows, preferred_element_typ...  7.8 us
  transfers between devices with their start and end apart: 4, of which 1 were waited for; matrix products, arithmetic and copies ran while one was open for 12% of the time, Pallas kernels for 18%

profile of v1, /device:TPU:0, one launch (start us, length us, event | category | flops | bytes accessed | tf_op | source)
XLA Modules:
  0.0 384.4 jit_solution(15660163356223117912)
XLA Ops:
  7.2 0.0 all-gather.4.cloned.1.call-start
  7.2 1.2 reshape.82
  8.4 0.1 copy.27
  8.5 12.1 %all_to_all.30 = bf16[42,4,1024]{2,0,1:T(8,128)(2,1)S(1)} all-to-all(bf16[42,4,1024]{2,0,1:T(8,128)(2,1)S(1)} %copy.27), channel_id=1, replica_groups=mesh['row'=8,'col'=4] {'col'}, dimensions={1} | all-to-all | bytes 688128 | tf_op jit(solution)/shard_map/all_to_all | solution.py:230
  20.6 0.8 reshape.83
  21.5 0.0 all-gather.4.cloned.1.call-update
  21.5 1.2 reshape.84
  22.7 0.9 copy.28
  23.5 3.5 all-to-all-start.1
  27.0 0.0 all-gather.6.cloned.1.call-start
  29.7 0.1 maximum_bitcast_fusion
  29.7 67.7 %all-gather = f32[32,1,4]{2,1,0:T(1,128)S(1)} all-gather(f32[1,1,4]{2,1,0:T(1,128)S(1)} %maximum_bitcast_fusion), channel_id=1, replica_groups=mesh['row'=8,'col'=4] {'row','col'}, dimensions={0}, use_global_device_ids=true | all-gather | bytes 528 | tf_op jit(solution)/shard_map/all_gather | solution.py:211
  97.5 0.1 copy.26
  97.5 0.0 all-to-all-done.1
  97.5 0.8 reshape.85
  98.4 0.0 all-gather.6.cloned.1.call-update
  98.4 0.0 reduce-scatter.2.cloned.1.call-start
  98.5 0.1 convert_reduce_fusion
  98.6 0.1 select_reduce_fusion.3
  98.7 0.2 select_reduce_fusion
  98.9 0.1 add_select_fusion
  99.0 0.1 select_n.17
  99.1 0.1 select_reduce_fusion.2
  99.2 0.1 select_reduce_fusion.1
  99.3 0.1 broadcast_in_dim.20
  99.4 0.1 mul.89
  99.5 6.1 %copy.29.refs_0_ = bf16[1024,1848]{1,0:T(8,128)(2,1)} copy(bf16[1024,1848]{0,1:T(8,128)(2,1)} %param.15) | data formatting | bytes 7569408 | tf_op args[6]
  105.6 6.1 %copy.30.refs_1_ = bf16[1024,1848]{1,0:T(8,128)(2,1)} copy(bf16[1024,1848]{0,1:T(8,128)(2,1)} %param.16) | data formatting | bytes 7569408 | tf_op args[7]
  111.7 0.0 all-gather.4.cloned.1.call-done
  111.7 6.6 %fusion.19.a_ref = bf16[1024,1024]{1,0:T(8,128)(2,1)} fusion(bf16[1344,1024]{1,0:T(8,128)(2,1)} %all-gather.4.cloned.1.call-done, f32[1344]{0:T(1024)S(1)} %mul.89, s32[1344]{0:T(1024)S(1)} %select_n.17), kind=kOutput, calls=%fused_computation.27 | convolution fusion | flops 2825125888 | bytes 4860416 | tf_op jit(solution)/shard_map/dot_general | solution.py:235
  118.3 67.6 %shard_map.120 = bf16[1024,1848]{1,0:T(8,128)(2,1)} custom-call(bf16[1024,1024]{1,0:T(8,128)(2,1)} %fusion.19.a_ref, bf16[1848,1024]{1,0:T(8,128)(2,1)} %refs_0_.2), custom_call_target="tpu_custom_call" | custom-call | flops 23253221376 | bytes 113541120 | tf_op jit(solution)/shard_map/pallas_call | solution.py:152
  186.0 0.0 all-gather.6.cloned.1.call-done
  186.0 6.4 %fusion.20.a_ref = bf16[1024,1024]{1,0:T(8,128)(2,1)} fusion(bf16[1344,1024]{1,0:T(8,128)(2,1)} %all-gather.6.cloned.1.call-done, s32[1344]{0:T(1024)S(1)} %select_n.17), kind=kOutput, calls=%fused_computation.28 | convolution fusion | flops 2820997120 | bytes 4855040 | tf_op jit(solution)/shard_map/dot_general | solution.py:235
  192.4 0.0 copy-start
  192.4 133.1 %shard_map.121 = (bf16[1024,1848]{1,0:T(8,128)(2,1)}, bf16[1024,1848]{1,0:T(8,128)(2,1)}) custom-call(bf16[1024,1024]{1,0:T(8,128)(2,1)} %fusion.20.a_ref, bf16[1024,1848]{1,0:T(8,128)(2,1)} %copy.29.refs_0_, bf16[1024,1848]{1,0:T(8,128)(2,1)} %copy.30.refs_1_), custom_call_target="tpu_custom_call" | custom-call | flops 46506442752 | bytes 227082240 | tf_op jit(solution)/shard_map/pallas_call | solution.py:152
  325.5 0.0 copy-done
  325.5 0.0 copy-start.6
  325.5 6.0 %fusion.3 = bf16[1024,1848]{1,0:T(8,128)(2,1)S(1)} fusion(bf16[1024,1848]{1,0:T(8,128)(2,1)} %get-tuple-element.8, bf16[1024,1848]{1,0:T(8,128)(2,1)S(1)} %copy-done, bf16[1024,1848]{1,0:T(8,128)(2,1)} %get-tuple-element.9), kind=kLoop, calls=%fused_computation.9 | loop fusion | flops 24600576 | bytes 15138816 | tf_op jit(solution)/shard_map/convert_element_type | solution.py:251
  331.6 0.0 copy-start.5
  331.6 1.9 copy-done.5
  333.5 0.0 copy-done.6
  333.5 0.0 copy-start.2
  333.5 0.0 copy-start.7
  333.5 4.5 %fusion.28 = f32[1024,1024]{1,0:T(8,128)S(1)} fusion(bf16[1024,1848]{1,0:T(8,128)(2,1)S(1)} %fusion.3, bf16[1024,1848]{0,1:T(8,128)(2,1)S(1)} %copy-done.6), kind=kOutput, calls=%fused_computation.54 | convolution fusion | flops 3875536896 | bytes 11763712 | tf_op jit(solution)/shard_map/dot_general | solution.py:263
  338.0 0.0 copy-done.2
  338.0 0.0 copy-done.7
  338.0 0.0 copy-start.8
  338.0 6.4 %add_convert_fusion = bf16[1024,1024]{1,0:T(8,128)(2,1)} fusion(f32[1024,1024]{1,0:T(8,128)S(1)} %fusion.28, bf16[1024,1848]{0,1:T(8,128)(2,1)S(1)} %copy-done.7, bf16[1024,1848]{1,0:T(8,128)(2,1)S(1)} %copy-done, bf16[1024,1848]{1,0:T(8,128)(2,1)S(1)} %copy-done.2), kind=kOutput, calls=%fused_computation.19 | convolution fusion | flops 3892772864 | bytes 17645568 | tf_op jit(solution)/shard_map/dot_general | solution.py:269
  344.4 0.0 reduce-scatter.2.cloned.1.call-update
  344.4 0.0 copy-done.8
  344.4 0.0 copy-start.3
  344.4 0.0 copy-start.4
  344.4 0.0 copy-start.9
  344.5 7.9 %convolution_convert_fusion.1 = bf16[1024,1848]{0,1:T(8,128)(2,1)} fusion(bf16[1024,1024]{1,0:T(8,128)(2,1)S(1)} %copy-done.8, bf16[1024,1848]{1,0:T(8,128)(2,1)} %copy-done.5), kind=kOutput, calls=%fused_computation.23 | convolution fusion | flops 3877429248 | bytes 9666560 | tf_op jit(solution)/shard_map/dot_general | solution.py:257
  352.4 0.0 copy-done.3
  352.4 0.0 copy-done.4
  352.4 0.0 copy-done.9
  352.4 0.0 copy-start.1
  352.4 7.8 %fusion.13 = bf16[1848,1024]{1,0:T(8,128)(2,1)} fusion(bf16[1024,1024]{1,0:T(8,128)(2,1)S(1)} %copy-done.9, bf16[1024,1848]{1,0:T(8,128)(2,1)S(1)} %copy-done.4, bf16[1024,1848]{1,0:T(8,128)(2,1)S(1)} %copy-done.3), kind=kOutput, calls=%fused_computation.21 | convolution fusion | flops 3892568064 | bytes 13451264 | tf_op jit(solution)/shard_map/dot_general | solution.py:254
  360.2 0.0 copy-done.1
  360.2 6.7 %convolution_convert_fusion = bf16[1024,1848]{0,1:T(8,128)(2,1)} fusion(bf16[1024,1024]{1,0:T(8,128)(2,1)S(1)} %copy-done.8, bf16[1024,1848]{1,0:T(8,128)(2,1)S(1)} %copy-done.1, bf16[1024,1848]{1,0:T(8,128)(2,1)S(1)} %copy-done.3), kind=kOutput, calls=%fused_computation.22 | convolution fusion | flops 3892568064 | bytes 13451264 | tf_op jit(solution)/shard_map/dot_general | solution.py:260
  366.9 11.0 %reduce-scatter.2.cloned.1.call-done = bf16[128,1024]{1,0:T(8,128)(2,1)} async-done(((bf16[1024,1024]{1,0:T(8,128)(2,1)}), bf16[128,1024]{1,0:T(8,128)(2,1)}) %reduce-scatter.2.cloned.1.call-update) | async-done | bytes 262160 | tf_op jit(solution)/shard_map/reduce_scatter | solution.py:266
  (6 shorter events, 0.1 us)
Async XLA Ops:
  7.2 104.6 %all-gather.4.cloned.1.call-start = ((), (), s32[]{:S(2)}) async-start(), calls=%async_computation.3 | async-start | bytes 3096576 | tf_op jit(solution)/shard_map/all_gather | solution.py:239
  23.5 74.0 %all-to-all-start.1 = ((bf16[42,4,1024]{2,0,1:T(8,128)(2,1)}), bf16[42,4,1024]{2,0,1:T(8,128)(2,1)S(1)}, u32[]{:S(2)}, u32[]{:S(2)}) async-start(bf16[42,4,1024]{2,0,1:T(8,128)(2,1)} %copy.28), calls=%async_computation.1 | async-start | bytes 786432 | tf_op jit(solution)/shard_map/all_to_all | solution.py:230
  27.0 159.0 %all-gather.6.cloned.1.call-start = ((), (), s32[]{:S(2)}) async-start(), calls=%async_computation.4 | async-start | bytes 3096576 | tf_op jit(solution)/shard_map/all_gather | solution.py:238
  98.4 279.5 %reduce-scatter.2.cloned.1.call-start = ((), (), s32[]{:S(2)}) async-start(), calls=%async_computation.5 | async-start | bytes 2359296 | tf_op jit(solution)/shard_map/reduce_scatter | solution.py:266
  192.4 133.1 %copy-start = (bf16[1024,1848]{1,0:T(8,128)(2,1)S(1)}, bf16[1024,1848]{1,0:T(8,128)(2,1)}, u32[]{:S(2)}) copy-start(bf16[1024,1848]{1,0:T(8,128)(2,1)} %shard_map.120) | copy-start | bytes 11354116
  325.5 7.9 %copy-start.6 = (bf16[1024,1848]{0,1:T(8,128)(2,1)S(1)}, bf16[1024,1848]{0,1:T(8,128)(2,1)}, u32[]{:S(2)}) copy-start(bf16[1024,1848]{0,1:T(8,128)(2,1)} %param.15) | copy-start | bytes 11354116
  331.6 1.9 copy-start.5
  333.5 4.5 %copy-start.2 = (bf16[1024,1848]{1,0:T(8,128)(2,1)S(1)}, bf16[1024,1848]{1,0:T(8,128)(2,1)}, u32[]{:S(2)}) copy-start(bf16[1024,1848]{1,0:T(8,128)(2,1)} %get-tuple-element.9) | copy-start | bytes 11354116
  333.5 4.5 %copy-start.7 = (bf16[1024,1848]{0,1:T(8,128)(2,1)S(1)}, bf16[1024,1848]{0,1:T(8,128)(2,1)}, u32[]{:S(2)}) copy-start(bf16[1024,1848]{0,1:T(8,128)(2,1)} %param.16) | copy-start | bytes 11354116
  338.0 6.5 %copy-start.8 = (bf16[1024,1024]{1,0:T(8,128)(2,1)S(1)}, bf16[1024,1024]{1,0:T(8,128)(2,1)}, u32[]{:S(2)}) copy-start(bf16[1024,1024]{1,0:T(8,128)(2,1)} %fusion.20.a_ref) | copy-start | bytes 6291460
  344.4 7.9 %copy-start.3 = (bf16[1024,1848]{1,0:T(8,128)(2,1)S(1)}, bf16[1024,1848]{1,0:T(8,128)(2,1)}, u32[]{:S(2)}) copy-start(bf16[1024,1848]{1,0:T(8,128)(2,1)} %get-tuple-element.9) | copy-start | bytes 11354116
  344.4 7.9 %copy-start.4 = (bf16[1024,1848]{1,0:T(8,128)(2,1)S(1)}, bf16[1024,1848]{1,0:T(8,128)(2,1)}, u32[]{:S(2)}) copy-start(bf16[1024,1848]{1,0:T(8,128)(2,1)} %get-tuple-element.8) | copy-start | bytes 11354116
  344.4 7.9 %copy-start.9 = (bf16[1024,1024]{1,0:T(8,128)(2,1)S(1)}, bf16[1024,1024]{1,0:T(8,128)(2,1)}, u32[]{:S(2)}) copy-start(bf16[1024,1024]{1,0:T(8,128)(2,1)} %fusion.19.a_ref) | copy-start | bytes 6291460
  352.4 7.8 %copy-start.1 = (bf16[1024,1848]{1,0:T(8,128)(2,1)S(1)}, bf16[1024,1848]{1,0:T(8,128)(2,1)}, u32[]{:S(2)}) copy-start(bf16[1024,1848]{1,0:T(8,128)(2,1)} %shard_map.120) | copy-start | bytes 11354116
Sparse Core Ops, SparseCore 0:
  21.6 34.5 all-gather.3
  98.5 30.6 all-gather.5
  344.5 33.2 reduce-scatter.1

commit v2 on v1

--- a/solution.py
+++ b/solution.py
@@ -34,7 +34,7 @@
     return jnp.sum(jnp.where(earlier, lengths[None, :], 0), 1)
 
 
-def square_kernel(count, transposed, a_ref, *refs):
+def square_kernel(count, a_ref, *refs):
     b_refs, o_refs = refs[:count], refs[count : 2 * count]
     parts, first_in, second_out, second_in = (
         refs[2 * count + i * count : 3 * count + i * count] for i in range(4)
@@ -82,7 +82,7 @@
 
     def phase_first(chunk, carry):
         block = a_ref[rows(chunk * CHUNK, CHUNK), :]
-        dims = (((1,), (1 if transposed else 0,)), ((), ()))
+        dims = (((1,), (1,)), ((), ()))
         for i in range(count):
             parts[i][rows(chunk * CHUNK, CHUNK), :] = lax.dot_general(
                 block, b_refs[i][...], dims, preferred_element_type=jnp.float32
@@ -144,13 +144,13 @@
         lax.fori_loop(0, chunks, phase, 0)
 
 
-def square_sum(a, bs, transposed, collective_id):
+def square_sum(a, bs, collective_id):
     tokens, depth = a.shape
-    units = bs[0].shape[0 if transposed else 1]
+    units = bs[0].shape[0]
     count = len(bs)
     shapes = (tokens, tokens // 2, tokens // 4, tokens // 4)
     return pl.pallas_call(
-        functools.partial(square_kernel, count, transposed),
+        functools.partial(square_kernel, count),
         out_shape=[jax.ShapeDtypeStruct((tokens, units), jnp.bfloat16)] * count,
         in_specs=[pl.BlockSpec(memory_space=pltpu.VMEM)] * (1 + count),
         out_specs=[pl.BlockSpec(memory_space=pltpu.VMEM)] * count,
@@ -169,10 +169,83 @@
     )(a, *bs)
 
 
-def column_sum(a, bs, transposed, collective_id):
+def table_kernel(mine_ref, all_ref, send_sem, recv_sem, own_sem):
+    row, col = lax.axis_index("row"), lax.axis_index("col")
+    row_count, col_count = lax.axis_size("row"), lax.axis_size("col")
+    barrier = pltpu.get_barrier_semaphore()
+
+    def col_peer(step):
+        return (row, lax.rem(col + step, col_count))
+
+    def row_peer(step):
+        return (lax.rem(row + step, row_count), col)
+
+    for step in range(1, col_count):
+        pl.semaphore_signal(barrier, inc=1, device_id=col_peer(step), device_id_type=MESH)
+    for step in range(1, row_count):
+        pl.semaphore_signal(barrier, inc=1, device_id=row_peer(step), device_id_type=MESH)
+    own = pltpu.make_async_copy(mine_ref, all_ref.at[row * col_count + col], own_sem)
+    own.start()
+    pl.semaphore_wait(barrier, col_count + row_count - 2)
+    copies = [
+        pltpu.make_async_remote_copy(
+            src_ref=mine_ref,
+            dst_ref=all_ref.at[row * col_count + col],
+            send_sem=send_sem.at[step],
+            recv_sem=recv_sem.at[step],
+            device_id=col_peer(step),
+            device_id_type=MESH,
+        )
+        for step in range(1, col_count)
+    ]
+    for copy in copies:
+        copy.start()
+    own.wait()
+    for copy in copies:
+        copy.wait_recv()
+    held = all_ref.at[pl.ds(row * col_count, col_count)]
+    onward = [
+        pltpu.make_async_remote_copy(
+            src_ref=held,
+            dst_ref=held,
+            send_sem=send_sem.at[col_count + step],
+            recv_sem=recv_sem.at[col_count + step],
+            device_id=row_peer(step),
+            device_id_type=MESH,
+        )
+        for step in range(1, row_count)
+    ]
+    for copy in onward:
+        copy.start()
+    for copy in onward:
+        copy.wait_recv()
+    for copy in copies + onward:
+        copy.wait_send()
+
+
+def gather_table(local):
+    row_count, col_count = lax.axis_size("row"), lax.axis_size("col")
+    devices = row_count * col_count
+    mine = jnp.pad(local, ((0, 0), (0, 128 - local.shape[1])))
+    every = pl.pallas_call(
+        table_kernel,
+        out_shape=jax.ShapeDtypeStruct((devices, 1, 128), jnp.float32),
+        in_specs=[pl.BlockSpec(memory_space=pltpu.VMEM)],
+        out_specs=pl.BlockSpec(memory_space=pltpu.VMEM),
+        scratch_shapes=[
+            pltpu.SemaphoreType.DMA((row_count + col_count,)),
+            pltpu.SemaphoreType.DMA((row_count + col_count,)),
+            pltpu.SemaphoreType.DMA,
+        ],
+        compiler_params=pltpu.CompilerParams(collective_id=2, has_side_effects=True),
+    )(mine)
+    return every[:, 0, : local.shape[1]]
+
+
+def column_sum(a, bs, collective_id):
     if lax.axis_size("col") == 4 and a.shape[0] % CHUNK == 0:
-        return square_sum(a, bs, transposed, collective_id)
-    dims = (((1,), (1 if transposed else 0,)), ((), ()))
+        return square_sum(a, bs, collective_id)
+    dims = (((1,), (1,)), ((), ()))
     return [
         lax.psum(
             lax.dot_general(a, b, dims, preferred_element_type=jnp.float32).astype(jnp.bfloat16),
@@ -208,7 +281,7 @@
         ],
         axis=1,
     )
-    table = lax.all_gather(local, ("row", "col"), axis=0, tiled=True)
+    table = gather_table(local)
     all_lengths = table[:, 0].astype(jnp.int32)
     all_owners = table[:, 1].astype(jnp.int32)
     all_prompts = table[:, 2].astype(jnp.int32)
@@ -234,15 +307,16 @@
     def repack(every):
         return jnp.dot(pick, every, preferred_element_type=jnp.float32).astype(jnp.bfloat16)
 
-    hidden_cols, table = lax.optimization_barrier((to_cols(roll_hidden), table))
+    hidden_cols, roll_cotangent = lax.optimization_barrier((to_cols(roll_hidden), roll_cotangent))
     hidden_all = lax.all_gather(hidden_cols, "row", axis=0, tiled=True)
     cotangent_all = lax.all_gather(to_cols(roll_cotangent), "row", axis=0, tiled=True)
     packed = repack(hidden_all)
-    gate, upval = column_sum(packed, (gate_weight, up_weight), False, 0)
+    gate, upval = column_sum(packed, (gate_weight.T, up_weight.T), 0)
+    slot_weights, gate, upval = lax.optimization_barrier((slot_weights, gate, upval))
     packed_grad = repack(
         (cotangent_all.astype(jnp.float32) * slot_weights[:, None]).astype(jnp.bfloat16)
     )
-    (grad_hidden,) = column_sum(packed_grad, (down_weight,), True, 1)
+    (grad_hidden,) = column_sum(packed_grad, (down_weight,), 1)
     gate, upval, grad_hidden = (v.astype(jnp.float32) for v in (gate, upval, grad_hidden))
     sig = jax.nn.sigmoid(gate)
     silu = gate * sig

time: 385 us -> 341 us (0.89)
  blocking collectives: 79.8 us -> 12.1 us
  Pallas kernels: 201 us -> 223 us
  waiting for transfers between devices: 11 us -> 23.6 us
  local copies, waits for them, and re-layouts: 19.5 us -> 8.07 us
    all_gather x1 -> x0, blocking collectives: 67.7 us -> none  [per_device(): table = lax.all_gather(local, ('row', 'col'), axis=0, tiled=True)]
    pallas_call x2 -> x3, Pallas kernels: 201 us -> 223 us  [the longest x2 212 us: square_sum(): pl.pallas_call(functools.partial(square_kernel, count), out_shape=[jax.Sh...]
    unnamed x22, local copies, waits for them, and re-layouts: 14.1 us -> 1.99 us
    all_to_all x1, waiting for transfers between devices: 0.01 us -> 6.58 us  [to_cols(): lax.all_to_all(blocks, 'col', split_axis=1, concat_axis=0, tiled=True)]
    all_gather x1, waiting for transfers between devices: 0.02 us -> 5.57 us  [per_device(): hidden_all = lax.all_gather(hidden_cols, 'row', axis=0, tiled=True)]
  transfers between devices with their start and end apart: 4 -> 4, of which waited for: 1 -> 3; matrix products, arithmetic and copies ran while one was open for 12% -> 10% of each run, Pallas kernels for 18% -> 44%
where the time goes in v2:
time: 341 us; the launch traced here: 340 us
  Pallas kernels  223 us (65%)
  matrix products  46.4 us (14%)
  waiting for transfers between devices  23.6 us (7%)
  between operations  16.6 us (5%)
  blocking collectives  12.1 us (4%)
  local copies, waits for them, and re-layouts  8.07 us (2%)
  other arithmetic  6.6 us (2%)
  starting transfers between devices  3.58 us (1%)
    pallas_call x2, Pallas kernels, square_sum(): pl.pallas_call(functools.partial(square_kernel, count), out_shape=[jax.Sh...  212 us
    dot_general x2, matrix products, repack(): jnp.dot(pick, every, preferred_element_type=jnp.float32)  12.9 us
    all_to_all x1, blocking collectives, to_cols(): lax.all_to_all(blocks, 'col', split_axis=1, concat_axis=0, tiled=True)  12.1 us
    reduce_scatter x1, waiting for transfers between devices, per_device(): lax.psum_scatter((term + lax.dot_general(grad_up_act, up_weight, contract...  11.4 us
    pallas_call x1, Pallas kernels, gather_table(): pl.pallas_call(table_kernel, out_shape=jax.ShapeDtypeStruct((devices, 1,...  11.2 us
    dot_general x1, matrix products, per_device(): lax.dot_general(packed, grad_gate_act, contract_rows, preferred_element_t...  7.89 us
    dot_general x1, matrix products, per_device(): lax.dot_general(hidden, packed_grad, contract_rows, preferred_element_typ...  7.79 us
  transfers between devices with their start and end apart: 4, of which 3 were waited for; matrix products, arithmetic and copies ran while one was open for 10% of the time, Pallas kernels for 44%

profile of v2, /device:TPU:0, one launch (start us, length us, event | category | flops | bytes accessed | tf_op | source)
XLA Modules:
  0.0 340.1 jit_solution(15879843010482527754)
XLA Ops:
  7.2 0.0 all-gather.5.cloned.1.call-start
  7.2 1.2 reshape.85
  8.4 0.1 copy.18
  8.5 12.1 %all_to_all.30 = bf16[42,4,1024]{2,0,1:T(8,128)(2,1)S(1)} all-to-all(bf16[42,4,1024]{2,0,1:T(8,128)(2,1)S(1)} %copy.18), channel_id=1, replica_groups=mesh['row'=8,'col'=4] {'col'}, dimensions={1} | all-to-all | bytes 688128 | tf_op jit(solution)/shard_map/all_to_all | solution.py:303
  20.6 0.8 reshape.86
  21.5 0.0 all-gather.5.cloned.1.call-update
  24.1 0.6 select_maximum_fusion.mine_ref
  24.7 11.2 %shard_map.120 = f32[32,1,128]{2,1,0:T(1,128)} custom-call(f32[1,128]{1,0:T(1,128)} %select_maximum_fusion.mine_ref), custom_call_target="tpu_custom_call" | custom-call | tf_op jit(solution)/shard_map/pallas_call | solution.py:230
  35.9 0.8 copy.17
  36.7 0.2 convert_reduce_fusion
  36.9 0.1 select_reduce_fusion.3
  37.0 0.1 select_reduce_fusion.2
  37.1 0.2 select_reduce_fusion
  37.3 0.1 add_select_fusion
  37.4 1.2 reshape.87
  38.6 0.9 copy.19
  39.4 3.5 %all-to-all-start.1 = ((bf16[42,4,1024]{2,0,1:T(8,128)(2,1)}), bf16[42,4,1024]{2,0,1:T(8,128)(2,1)S(1)}, u32[]{:S(2)}, u32[]{:S(2)}) async-start(bf16[42,4,1024]{2,0,1:T(8,128)(2,1)} %copy.19), calls=%async_computation.1 | async-start | bytes 786432 | tf_op jit(solution)/shard_map/all_to_all | solution.py:303
  42.9 0.0 all-gather.3.cloned.1.call-start
  43.0 0.1 select_reduce_fusion.1
  43.0 0.1 select_n.17
  43.2 0.1 broadcast_in_dim.20
  43.2 0.1 reshape.89
  43.3 6.6 %all-to-all-done.1 = bf16[42,4,1024]{2,0,1:T(8,128)(2,1)S(1)} async-done(((bf16[42,4,1024]{2,0,1:T(8,128)(2,1)}), bf16[42,4,1024]{2,0,1:T(8,128)(2,1)S(1)}, u32[]{:S(2)}, u32[]{:S(2)}) %all-to-all-start.1) | async-done | bytes 344096 | tf_op jit(solution)/shard_map/all_to_all | solution.py:303
  49.9 0.8 reshape.88
  50.8 0.0 all-gather.3.cloned.1.call-update
  50.8 0.0 reduce-scatter.2.cloned.1.call-start
  50.8 5.6 %all-gather.5.cloned.1.call-done = bf16[1344,1024]{1,0:T(8,128)(2,1)} async-done(((bf16[168,1024]{1,0:T(8,128)(2,1)}), bf16[1344,1024]{1,0:T(8,128)(2,1)}) %all-gather.5.cloned.1.call-update) | async-done | bytes 2752528 | tf_op jit(solution)/shard_map/all_gather | solution.py:311
  56.4 6.3 %fusion.19.a_ref = bf16[1024,1024]{1,0:T(8,128)(2,1)} fusion(bf16[1344,1024]{1,0:T(8,128)(2,1)} %all-gather.5.cloned.1.call-done, s32[1344]{0:T(1024)S(1)} %select_n.17), kind=kOutput, calls=%fused_computation.27 | convolution fusion | flops 2820997120 | bytes 4855040 | tf_op jit(solution)/shard_map/dot_general | solution.py:308
  62.7 140.1 %shard_map.121 = (bf16[1024,1848]{1,0:T(8,128)(2,1)}, bf16[1024,1848]{1,0:T(8,128)(2,1)}) custom-call(bf16[1024,1024]{1,0:T(8,128)(2,1)} %fusion.19.a_ref, bf16[1848,1024]{1,0:T(8,128)(2,1)} %bitcast.60, bf16[1848,1024]{1,0:T(8,128)(2,1)} %bitcast.61), custom_call_target="tpu_custom_call" | custom-call | flops 46506442752 | bytes 227082240 | tf_op jit(solution)/shard_map/pallas_call | solution.py:152
  202.8 0.0 all-gather.3.cloned.1.call-done
  202.9 6.6 %fusion.20.a_ref = bf16[1024,1024]{1,0:T(8,128)(2,1)} fusion(bf16[1344,1024]{1,0:T(8,128)(2,1)} %all-gather.3.cloned.1.call-done, f32[1344]{0:T(1024)S(1)} %reshape.89, s32[1344]{0:T(1024)S(1)} %select_n.17), kind=kOutput, calls=%fused_computation.28 | convolution fusion | flops 2825125888 | bytes 4860416 | tf_op jit(solution)/shard_map/dot_general | solution.py:308
  209.4 0.0 copy-start
  209.4 0.0 copy-start.2
  209.4 71.9 %shard_map.122 = bf16[1024,1848]{1,0:T(8,128)(2,1)} custom-call(bf16[1024,1024]{1,0:T(8,128)(2,1)} %fusion.20.a_ref, bf16[1848,1024]{1,0:T(8,128)(2,1)} %refs_0_.1), custom_call_target="tpu_custom_call" | custom-call | flops 23253221376 | bytes 113541120 | tf_op jit(solution)/shard_map/pallas_call | solution.py:152
  281.3 0.0 copy-done
  281.3 0.0 copy-done.2
  281.3 0.0 copy-start.7
  281.3 5.3 %fusion.3 = bf16[1024,1848]{1,0:T(8,128)(2,1)S(1)} fusion(bf16[1024,1848]{1,0:T(8,128)(2,1)S(1)} %copy-done.2, bf16[1024,1848]{1,0:T(8,128)(2,1)} %shard_map.122, bf16[1024,1848]{1,0:T(8,128)(2,1)S(1)} %copy-done), kind=kLoop, calls=%fused_computation.9 | loop fusion | flops 24600576 | bytes 15138816 | tf_op jit(solution)/shard_map/convert_element_type | solution.py:325
  286.6 0.0 copy-start.6
  286.6 1.9 copy-done.6
  288.6 0.0 copy-done.7
  288.6 0.0 copy-start.4
  288.6 0.0 copy-start.8
  288.6 4.5 %fusion.28 = f32[1024,1024]{1,0:T(8,128)S(1)} fusion(bf16[1024,1848]{1,0:T(8,128)(2,1)S(1)} %fusion.3, bf16[1024,1848]{0,1:T(8,128)(2,1)S(1)} %copy-done.7), kind=kOutput, calls=%fused_computation.57 | convolution fusion | flops 3875536896 | bytes 11763712 | tf_op jit(solution)/shard_map/dot_general | solution.py:337
  293.0 0.0 copy-done.4
  293.1 0.0 copy-done.8
  293.1 0.0 copy-start.9
  293.1 6.6 %add_convert_fusion = bf16[1024,1024]{1,0:T(8,128)(2,1)} fusion(f32[1024,1024]{1,0:T(8,128)S(1)} %fusion.28, bf16[1024,1848]{0,1:T(8,128)(2,1)S(1)} %copy-done.8, bf16[1024,1848]{1,0:T(8,128)(2,1)S(1)} %copy-done.4, bf16[1024,1848]{1,0:T(8,128)(2,1)S(1)} %copy-done), kind=kOutput, calls=%fused_computation.19 | convolution fusion | flops 3892772864 | bytes 17645568 | tf_op jit(solution)/shard_map/dot_general | solution.py:343
  299.7 0.0 reduce-scatter.2.cloned.1.call-update
  299.7 0.0 copy-done.9
  299.7 0.0 copy-start.1
  299.7 0.0 copy-start.3
  299.7 0.0 copy-start.10
  299.7 7.9 %convolution_convert_fusion.1 = bf16[1024,1848]{0,1:T(8,128)(2,1)} fusion(bf16[1024,1024]{1,0:T(8,128)(2,1)S(1)} %copy-done.9, bf16[1024,1848]{1,0:T(8,128)(2,1)} %copy-done.6), kind=kOutput, calls=%fused_computation.23 | convolution fusion | flops 3877429248 | bytes 9666560 | tf_op jit(solution)/shard_map/dot_general | solution.py:331
  307.6 0.0 copy-done.1
  307.6 0.0 copy-done.3
  307.6 0.0 copy-done.10
  307.6 0.0 copy-start.5
  307.7 7.8 %fusion.13 = bf16[1848,1024]{1,0:T(8,128)(2,1)} fusion(bf16[1024,1024]{1,0:T(8,128)(2,1)S(1)} %copy-done.10, bf16[1024,1848]{1,0:T(8,128)(2,1)S(1)} %copy-done.3, bf16[1024,1848]{1,0:T(8,128)(2,1)S(1)} %copy-done.1), kind=kOutput, calls=%fused_computation.21 | convolution fusion | flops 3892568064 | bytes 13451264 | tf_op jit(solution)/shard_map/dot_general | solution.py:328
  315.4 0.0 copy-done.5
  315.4 6.7 %convolution_convert_fusion = bf16[1024,1848]{0,1:T(8,128)(2,1)} fusion(bf16[1024,1024]{1,0:T(8,128)(2,1)S(1)} %copy-done.9, bf16[1024,1848]{1,0:T(8,128)(2,1)S(1)} %copy-done.5, bf16[1024,1848]{1,0:T(8,128)(2,1)S(1)} %copy-done.1), kind=kOutput, calls=%fused_computation.22 | convolution fusion | flops 3892568064 | bytes 13451264 | tf_op jit(solution)/shard_map/dot_general | solution.py:334
  322.2 11.4 %reduce-scatter.2.cloned.1.call-done = bf16[128,1024]{1,0:T(8,128)(2,1)} async-done(((bf16[1024,1024]{1,0:T(8,128)(2,1)}), bf16[128,1024]{1,0:T(8,128)(2,1)}) %reduce-scatter.2.cloned.1.call-update) | async-done | bytes 262160 | tf_op jit(solution)/shard_map/reduce_scatter | solution.py:340
  (6 shorter events, 0.1 us)
Async XLA Ops:
  7.2 49.2 %all-gather.5.cloned.1.call-start = ((), (), s32[]{:S(2)}) async-start(), calls=%async_computation.4 | async-start | bytes 3096576 | tf_op jit(solution)/shard_map/all_gather | solution.py:311
  39.4 10.5 %all-to-all-start.1 = ((bf16[42,4,1024]{2,0,1:T(8,128)(2,1)}), bf16[42,4,1024]{2,0,1:T(8,128)(2,1)S(1)}, u32[]{:S(2)}, u32[]{:S(2)}) async-start(bf16[42,4,1024]{2,0,1:T(8,128)(2,1)} %copy.19), calls=%async_computation.1 | async-start | bytes 786432 | tf_op jit(solution)/shard_map/all_to_all | solution.py:303
  42.9 159.9 %all-gather.3.cloned.1.call-start = ((), (), s32[]{:S(2)}) async-start(), calls=%async_computation.3 | async-start | bytes 3096576 | tf_op jit(solution)/shard_map/all_gather | solution.py:312
  50.8 282.7 %reduce-scatter.2.cloned.1.call-start = ((), (), s32[]{:S(2)}) async-start(), calls=%async_computation.5 | async-start | bytes 2359296 | tf_op jit(solution)/shard_map/reduce_scatter | solution.py:340
  209.4 71.9 %copy-start = (bf16[1024,1848]{1,0:T(8,128)(2,1)S(1)}, bf16[1024,1848]{1,0:T(8,128)(2,1)}, u32[]{:S(2)}) copy-start(bf16[1024,1848]{1,0:T(8,128)(2,1)} %get-tuple-element.17) | copy-start | bytes 11354116
  209.4 71.9 %copy-start.2 = (bf16[1024,1848]{1,0:T(8,128)(2,1)S(1)}, bf16[1024,1848]{1,0:T(8,128)(2,1)}, u32[]{:S(2)}) copy-start(bf16[1024,1848]{1,0:T(8,128)(2,1)} %get-tuple-element.16) | copy-start | bytes 11354116
  281.3 7.2 %copy-start.7 = (bf16[1024,1848]{0,1:T(8,128)(2,1)S(1)}, bf16[1024,1848]{0,1:T(8,128)(2,1)}, u32[]{:S(2)}) copy-start(bf16[1024,1848]{0,1:T(8,128)(2,1)} %param.15) | copy-start | bytes 11354116
  286.6 1.9 copy-start.6
  288.6 4.5 %copy-start.4 = (bf16[1024,1848]{1,0:T(8,128)(2,1)S(1)}, bf16[1024,1848]{1,0:T(8,128)(2,1)}, u32[]{:S(2)}) copy-start(bf16[1024,1848]{1,0:T(8,128)(2,1)} %shard_map.122) | copy-start | bytes 11354116
  288.6 4.5 %copy-start.8 = (bf16[1024,1848]{0,1:T(8,128)(2,1)S(1)}, bf16[1024,1848]{0,1:T(8,128)(2,1)}, u32[]{:S(2)}) copy-start(bf16[1024,1848]{0,1:T(8,128)(2,1)} %param.16) | copy-start | bytes 11354116
  293.1 6.6 %copy-start.9 = (bf16[1024,1024]{1,0:T(8,128)(2,1)S(1)}, bf16[1024,1024]{1,0:T(8,128)(2,1)}, u32[]{:S(2)}) copy-start(bf16[1024,1024]{1,0:T(8,128)(2,1)} %fusion.19.a_ref) | copy-start | bytes 6291460
  299.7 7.9 %copy-start.1 = (bf16[1024,1848]{1,0:T(8,128)(2,1)S(1)}, bf16[1024,1848]{1,0:T(8,128)(2,1)}, u32[]{:S(2)}) copy-start(bf16[1024,1848]{1,0:T(8,128)(2,1)} %get-tuple-element.17) | copy-start | bytes 11354116
  299.7 7.9 %copy-start.3 = (bf16[1024,1848]{1,0:T(8,128)(2,1)S(1)}, bf16[1024,1848]{1,0:T(8,128)(2,1)}, u32[]{:S(2)}) copy-start(bf16[1024,1848]{1,0:T(8,128)(2,1)} %get-tuple-element.16) | copy-start | bytes 11354116
  299.7 7.9 %copy-start.10 = (bf16[1024,1024]{1,0:T(8,128)(2,1)S(1)}, bf16[1024,1024]{1,0:T(8,128)(2,1)}, u32[]{:S(2)}) copy-start(bf16[1024,1024]{1,0:T(8,128)(2,1)} %fusion.20.a_ref) | copy-start | bytes 6291460
  307.6 7.8 %copy-start.5 = (bf16[1024,1848]{1,0:T(8,128)(2,1)S(1)}, bf16[1024,1848]{1,0:T(8,128)(2,1)}, u32[]{:S(2)}) copy-start(bf16[1024,1848]{1,0:T(8,128)(2,1)} %shard_map.122) | copy-start | bytes 11354116
Sparse Core Ops, SparseCore 0:
  21.6 34.7 all-gather.4
  58.6 33.9 all-gather.2
  299.8 33.6 reduce-scatter.1
